TPU v7x, 32 devices: a whole 2x2x4 slice. The times are simulated.
32 devices in a mesh: feat: 8 (over z, y), tok: 4 (over x, core).
Axes of the slice: x: 2, y: 2, z: 4, core: 2. Of those that a mesh axis runs over, the one named last changes fastest.
Arguments:
- activations: bfloat16 [2048, 7168], P('tok', 'feat'), may hold values from -6 to 6
- top_lists: int32 [2048, 64], P('tok'), may hold values from 0 to 4095, all different within a row
- encoder_weight: bfloat16 [7168, 4096], P(None, 'feat'), may hold values from -0.0625 to 0.0625
- encoder_bias: float32 [4096], P('feat'), may hold values from -3 to 3
- decoder_weight: bfloat16 [7168, 4096], P(None, 'feat'), may hold values from -0.125 to 0.125
- decoder_bias: float32 [7168], replicated, may hold values from -3 to 3
Outputs:
- encoder_grad: float32 [7168, 4096], P('tok', 'feat')
- decoder_grad: float32 [7168, 4096], P('tok', 'feat')
All inputs are finite; a program needn't handle non-finite values.
Results may differ from a plain program's by a relative error of at most 0.004.
Values may be sent and summed in bfloat16 or wider, within the bound.
A program may use at most 128 MiB of HBM per device.

v0:
```python
import jax
import jax.numpy as jnp
from jax import lax
from jax.sharding import PartitionSpec as P


def contract_rows(left, right):
    return lax.dot_general(
        left, right, (((0,), (0,)), ((), ())), preferred_element_type=jnp.float32
    )


def body(activations, top_lists, encoder_weight, encoder_bias, decoder_weight, decoder_bias):
    group_rows = activations.shape[0]
    feat_dev = encoder_weight.shape[1]
    shards = lax.axis_size("feat")
    owner = lax.axis_index("feat")
    row_share = group_rows // shards
    gathered = lax.all_gather(activations, "feat", axis=1, tiled=True)
    encoded = jnp.dot(gathered, encoder_weight, preferred_element_type=jnp.float32) + encoder_bias
    local_ids = top_lists - owner * feat_dev
    inside = (local_ids >= 0) & (local_ids < feat_dev)
    column = jnp.where(inside, local_ids, feat_dev)
    row_ids = jnp.arange(group_rows, dtype=jnp.int32)[:, None]
    chosen = (
        jnp.zeros((group_rows, feat_dev), jnp.float32).at[row_ids, column].set(1.0, mode="drop")
    )
    codes = jnp.where(chosen > 0.0, encoded, 0.0).astype(jnp.bfloat16)
    rebuilt = lax.psum_scatter(
        lax.dot_general(
            codes, decoder_weight, (((1,), (1,)), ((), ())), preferred_element_type=jnp.float32
        ),
        "feat",
        scatter_dimension=0,
        tiled=True,
    )
    own_rows = lax.dynamic_slice_in_dim(gathered, owner * row_share, row_share, 0)
    error_rows = (rebuilt + decoder_bias - own_rows.astype(jnp.float32)).astype(jnp.bfloat16)
    error = lax.all_gather(error_rows, "feat", axis=0, tiled=True)
    pulled = jnp.dot(error, decoder_weight, preferred_element_type=jnp.float32)
    code_grads = jnp.where(chosen > 0.0, pulled, 0.0).astype(jnp.bfloat16)
    input_cols, error_cols = (
        lax.all_to_all(gathered, "tok", split_axis=1, concat_axis=0, tiled=True),
        lax.all_to_all(error, "tok", split_axis=1, concat_axis=0, tiled=True),
    )
    grads_all, codes_all = (
        lax.all_gather(code_grads, "tok", axis=0, tiled=True),
        lax.all_gather(codes, "tok", axis=0, tiled=True),
    )
    encoder_grad = contract_rows(input_cols, grads_all)
    decoder_grad = contract_rows(error_cols, codes_all)
    return (encoder_grad, decoder_grad)


def solution(mesh):
    return jax.shard_map(
        body,
        mesh=mesh,
        in_specs=(
            P("tok", "feat"),
            P("tok", None),
            P(None, "feat"),
            P("feat"),
            P(None, "feat"),
            P(),
        ),
        out_specs=(P("tok", "feat"), P("tok", "feat")),
        check_vma=False,
    )
```

profile of v0, /device:TPU:0, one launch (start us, length us, event | category | flops | bytes accessed | tf_op | source)
XLA Modules:
  0.0 639.1 jit_solution(12103646338569349608)
XLA Ops:
  7.2 0.0 all-gather.5.cloned.1.call-start
  7.2 0.7 all-gather.5.cloned.1.call-update
  7.9 0.0 reduce-scatter.2.cloned.1.call-start
  7.9 0.9 fusion.5
  8.9 0.1 and_reduce_fusion
  9.0 0.8 multiply_reduce_fusion
  9.8 0.1 copy.12
  9.9 0.1 reshape.20
  10.0 120.3 %scatter_custom_fusion = f32[262144]{0:T(1024)S(1)} fusion(s32[32768]{0:T(1024)S(1)} %reshape.20, f32[32768]{0:T(1024)S(1)} %broadcast.30, f32[]{:T(128)} %constant.7.clone.1), kind=kCustom, calls=%fused_computation.11 | custom fusion | bytes 1048580
  130.3 0.1 broadcast_compare_fusion
  130.5 0.4 reshape.19
  130.8 0.0 all-gather.5.cloned.1.call-done
  130.9 9.1 %fusion.1 = bf16[512,512]{1,0:T(8,128)(2,1)S(1)} fusion(pred[512,512]{1,0:T(32,128)(4,1)S(1)} %reshape.19, bf16[512,7168]{1,0:T(8,128)(2,1)} %all-gather.5.cloned.1.call-done, bf16[7168,512]{1,0:T(8,128)(2,1)} %param.8, f32[512]{0:T(512)} %param.9), kind=kOutput, calls=%fused_computation.8 | convolution fusion | flops 3758882816 | bytes 15468544 | tf_op jit(solution)/shard_map/dot_general | solution.py:20
  140.0 10.5 %fusion.6 = f32[512,7168]{1,0:T(8,128)} fusion(bf16[512,512]{1,0:T(8,128)(2,1)S(1)} %fusion.1, bf16[7168,512]{1,0:T(8,128)(2,1)} %param.10), kind=kOutput, calls=%fused_computation.19 | convolution fusion | flops 3758096384 | bytes 22544384 | tf_op jit(solution)/shard_map/dot_general | solution.py:30
  150.6 0.0 all-gather.7.cloned.1.call-start
  150.6 239.5 %reduce-scatter.2.cloned.1.call-done = f32[64,7168]{1,0:T(8,128)} async-done(((f32[512,7168]{1,0:T(8,128)}), f32[64,7168]{1,0:T(8,128)}) %reduce-scatter.2.cloned.1.call-update) | async-done | bytes 1835024 | tf_op jit(solution)/shard_map/reduce_scatter | solution.py:29
  390.1 2.9 subtract_convert_fusion
  393.0 6.6 %copy.21 = bf16[64,4,8,1792]{3,2,0,1:T(8,128)(2,1)} copy(bf16[64,4,8,1792]{3,2,1,0:T(8,128)(2,1)} %bitcast.30) | data formatting | bytes 14680064 | tf_op jit(solution)/shard_map/all_to_all | solution.py:43
  399.6 5.7 all-to-all-start
  405.3 0.0 all-gather.9.cloned.1.call-start
  405.4 98.4 %all-gather.7.cloned.1.call-done = bf16[512,7168]{1,0:T(8,128)(2,1)} async-done(((bf16[64,7168]{1,0:T(8,128)(2,1)}), bf16[512,7168]{1,0:T(8,128)(2,1)}) %all-gather.7.cloned.1.call-update) | async-done | bytes 7340048 | tf_op jit(solution)/shard_map/all_gather | solution.py:39
  503.8 9.9 %fusion.2 = bf16[512,512]{1,0:T(8,128)(2,1)} fusion(pred[512,512]{1,0:T(32,128)(4,1)S(1)} %reshape.19, bf16[512,7168]{1,0:T(8,128)(2,1)} %all-gather.7.cloned.1.call-done, bf16[7168,512]{1,0:T(8,128)(2,1)} %param.10), kind=kOutput, calls=%fused_computation.9 | convolution fusion | flops 3758620672 | bytes 15466496 | tf_op jit(solution)/shard_map/dot_general | solution.py:40
  513.7 6.6 %copy.20 = bf16[64,4,8,1792]{3,2,0,1:T(8,128)(2,1)} copy(bf16[64,4,8,1792]{3,2,1,0:T(8,128)(2,1)} %bitcast.31) | data formatting | bytes 14680064 | tf_op jit(solution)/shard_map/all_to_all | solution.py:44
  520.3 5.4 all-to-all-start.1
  525.8 0.2 all-gather.11.cloned.1.call-start
  526.0 0.4 all-gather.11.cloned.1.call-update
  526.4 12.4 %all-gather.9.cloned.1.call-done = bf16[2048,512]{1,0:T(8,128)(2,1)} async-done(((bf16[512,512]{1,0:T(8,128)(2,1)}), bf16[2048,512]{1,0:T(8,128)(2,1)}) %all-gather.9.cloned.1.call-update) | async-done | bytes 2097168 | tf_op jit(solution)/shard_map/all_gather | solution.py:47
  538.8 9.6 %convolution_bitcast_fusion = f32[1792,512]{0,1:T(8,128)} fusion(bf16[2048,512]{1,0:T(8,128)(2,1)} %all-gather.9.cloned.1.call-done, bf16[2048,1792]{1,0:T(8,128)(2,1)} %bitcast.2), kind=kOutput, calls=%fused_computation.3 | convolution fusion | flops 3758096384 | bytes 13107200 | tf_op jit(solution)/shard_map/dot_general | solution.py:8
  548.4 5.2 copy.15
  553.6 23.4 %all-gather.11.cloned.1.call-done = bf16[2048,512]{1,0:T(8,128)(2,1)} async-done(((bf16[512,512]{1,0:T(8,128)(2,1)}), bf16[2048,512]{1,0:T(8,128)(2,1)}) %all-gather.11.cloned.1.call-update) | async-done | bytes 2097168 | tf_op jit(solution)/shard_map/all_gather | solution.py:48
  577.0 46.0 %all-to-all-done.1 = bf16[512,4,1792]{2,0,1:T(8,128)(2,1)} async-done(((bf16[512,4,1792]{2,0,1:T(8,128)(2,1)}), bf16[512,4,1792]{2,0,1:T(8,128)(2,1)}, u32[]{:S(2)}, u32[]{:S(2)}) %all-to-all-start.1) | async-done | bytes 7340064 | tf_op jit(solution)/shard_map/all_to_all | solution.py:44
  623.1 9.5 %fusion.7 = f32[1792,512]{1,0:T(8,128)} fusion(bf16[2048,1792]{1,0:T(8,128)(2,1)} %bitcast.5, bf16[2048,512]{1,0:T(8,128)(2,1)} %all-gather.11.cloned.1.call-done), kind=kOutput, calls=%fused_computation.20 | convolution fusion | flops 3758096384 | bytes 13107200 | tf_op jit(solution)/shard_map/dot_general | solution.py:8
  (11 shorter events, 0.1 us)
Async XLA Ops:
  7.2 123.7 %all-gather.5.cloned.1.call-start = ((), (), s32[]{:S(2)}) async-start(), calls=%async_computation.3 | async-start | bytes 8257536 | tf_op jit(solution)/shard_map/all_gather | solution.py:19
  7.9 382.2 %reduce-scatter.2.cloned.1.call-start = ((), (), s32[]{:S(2)}) async-start(), calls=%async_computation.4 | async-start | bytes 16515072 | tf_op jit(solution)/shard_map/reduce_scatter | solution.py:29
  140.0 10.5 %copy-start = (bf16[512,512]{1,0:T(8,128)(2,1)}, bf16[512,512]{1,0:T(8,128)(2,1)S(1)}, u32[]{:S(2)}) copy-start(bf16[512,512]{1,0:T(8,128)(2,1)S(1)} %fusion.1) | copy-start | bytes 1572868
  150.5 239.6 %copy-start.1 = (f32[7168]{0:T(1024)S(1)}, f32[7168]{0:T(1024)}, u32[]{:S(2)}) copy-start(f32[7168]{0:T(1024)} %param.11) | copy-start | bytes 86020
  150.6 353.2 %all-gather.7.cloned.1.call-start = ((), (), s32[]{:S(2)}) async-start(), calls=%async_computation.5 | async-start | bytes 8257536 | tf_op jit(solution)/shard_map/all_gather | solution.py:39
  399.6 120.8 %all-to-all-start = ((bf16[512,4,1792]{2,0,1:T(8,128)(2,1)}), bf16[512,4,1792]{2,0,1:T(8,128)(2,1)}, u32[]{:S(2)}, u32[]{:S(2)}) async-start(bf16[512,4,1792]{2,0,1:T(8,128)(2,1)} %bitcast.29), calls=%async_computation.1 | async-start | bytes 14680064 | tf_op jit(solution)/shard_map/all_to_all | solution.py:43
  405.3 133.5 %all-gather.9.cloned.1.call-start = ((), (), s32[]{:S(2)}) async-start(), calls=%async_computation.6 | async-start | bytes 2621440 | tf_op jit(solution)/shard_map/all_gather | solution.py:47
  520.3 102.7 %all-to-all-start.1 = ((bf16[512,4,1792]{2,0,1:T(8,128)(2,1)}), bf16[512,4,1792]{2,0,1:T(8,128)(2,1)}, u32[]{:S(2)}, u32[]{:S(2)}) async-start(bf16[512,4,1792]{2,0,1:T(8,128)(2,1)} %bitcast.28), calls=%async_computation.2 | async-start | bytes 14680064 | tf_op jit(solution)/shard_map/all_to_all | solution.py:44
  525.8 51.2 %all-gather.11.cloned.1.call-start = ((), (), s32[]{:S(2)}) async-start(), calls=%async_computation.7 | async-start | bytes 2621440 | tf_op jit(solution)/shard_map/all_gather | solution.py:48
Sparse Core Ops, SparseCore 0:
  10.2 113.9 all-gather.4
  150.7 239.3 reduce-scatter.1
  393.1 110.5 all-gather.6
  513.8 24.9 all-gather.8
  540.2 36.7 all-gather.10
where the time goes:
time: 640 us; the launch traced here: 639 us
  waiting for transfers between devices  421 us (66%)
  local copies, waits for them, and re-layouts  139 us (22%)
  matrix products  48.7 us (8%)
  between operations  13.9 us (2%)
  starting transfers between devices  11.5 us (2%)
    reduce_scatter x1, waiting for transfers between devices, body(): lax.psum_scatter(lax.dot_general(codes, decoder_weight, (((1,), (1,)), ((...  240 us
    unnamed x9, local copies, waits for them, and re-layouts  126 us
    all_gather x1, waiting for transfers between devices, body(): error = lax.all_gather(error_rows, 'feat', axis=0, tiled=True)  98.4 us
    all_to_all x1, waiting for transfers between devices, body(): lax.all_to_all(error, 'tok', split_axis=1, concat_axis=0, tiled=True)  46 us
    all_gather x1, waiting for transfers between devices, body(): lax.all_gather(codes, 'tok', axis=0, tiled=True)  23.4 us
    dot_general x2, matrix products, contract_rows(): lax.dot_general(left, right, (((0,), (0,)), ((), ())), preferred_element_...  19.1 us
  transfers between devices with their start and end apart: 7, of which 5 were waited for; matrix products, arithmetic and copies ran while one was open for 25% of the time, Pallas kernels for 0%

commit v1 on v0

v1 whole, which is shorter than its diff:
```python
import functools

import jax
import jax.numpy as jnp
from jax import lax
from jax.experimental import pallas as pl
from jax.experimental.pallas import tpu as pltpu
from jax.sharding import PartitionSpec as P

ROWS = 128


def pick(values, lanes):
    return jnp.take_along_axis(values, lanes, axis=1, mode="promise_in_bounds")


def place_kernel(width, ids_ref, out_ref):
    rows, top = ids_ref.shape[1:]
    chunks = out_ref.shape[2] // width
    base = pl.program_id(0) * top
    lane = lax.broadcasted_iota(jnp.int32, (8, width), 1)

    def group(step, carry):
        at = pl.ds(pl.multiple_of(step * 8, 8), 8)
        ids = ids_ref[0, at, :]
        found = [jnp.full((8, width), -1, jnp.int32)] * chunks
        for k in range(top):
            relative = jnp.broadcast_to(ids[:, k : k + 1], (8, width)) - lane
            found = [jnp.where(relative == c * width, k, found[c]) for c in range(chunks)]
        for c in range(chunks):
            out_ref[0, at, c * width : (c + 1) * width] = jnp.where(
                found[c] >= 0, found[c] + base, -1
            )
        return carry

    lax.fori_loop(0, rows // 8, group, 0)


def place(ids, features, width):
    packs, rows, top = ids.shape
    return pl.pallas_call(
        functools.partial(place_kernel, width),
        grid=(packs, rows // ROWS),
        in_specs=[pl.BlockSpec((1, ROWS, top), lambda h, i: (h, i, 0))],
        out_specs=pl.BlockSpec((1, ROWS, features), lambda h, i: (h, i, 0)),
        out_shape=jax.ShapeDtypeStruct((packs, rows, features), jnp.int32),
        cost_estimate=pl.CostEstimate(
            flops=packs * rows * top * features * 20, bytes_accessed=packs * rows * features * 4,
            transcendentals=0,
        ),
        name="place",
    )(ids)


def project_kernel(width, rows_ref, weight_ref, ids_ref, bias_ref, out_ref):
    packs, rows, depth = rows_ref.shape
    chunks = weight_ref.shape[1] // width
    total = jnp.zeros((rows, width), jnp.float32)
    for h in range(packs):
        ids = ids_ref[h]
        chunk = lax.shift_right_arithmetic(ids, width.bit_length() - 1)
        lanes = lax.bitwise_and(ids, width - 1)
        for pair in range(0, chunks, 2):
            cols = slice(pair * width, (pair + 2) * width)
            product = jnp.dot(
                rows_ref[h], weight_ref[:, cols], preferred_element_type=jnp.float32
            ) + bias_ref[:, cols]
            for c in range(2):
                got = pick(product[:, c * width : (c + 1) * width], lanes)
                total = jnp.where(chunk == pair + c, got, total)
    out_ref[...] = total


def project(rows, weight, ids, bias, width):
    packs, count, depth = rows.shape
    features = weight.shape[1]
    return pl.pallas_call(
        functools.partial(project_kernel, width),
        grid=(count // ROWS,),
        in_specs=[
            pl.BlockSpec((packs, ROWS, depth), lambda i: (0, i, 0)),
            pl.BlockSpec((depth, features), lambda i: (0, 0)),
            pl.BlockSpec((packs, ROWS, width), lambda i: (0, i, 0)),
            pl.BlockSpec((1, features), lambda i: (0, 0)),
        ],
        out_specs=pl.BlockSpec((ROWS, width), lambda i: (i, 0)),
        out_shape=jax.ShapeDtypeStruct((count, width), jnp.float32),
        cost_estimate=pl.CostEstimate(
            flops=2 * packs * count * depth * features,
            bytes_accessed=rows.size * 2 + weight.size * 2, transcendentals=0,
        ),
        name="project",
    )(rows, weight, ids, bias)


def spread_kernel(width, packed_ref, place_ref, out_ref):
    packed = packed_ref[...]
    for h in range(place_ref.shape[0]):
        for c in range(place_ref.shape[2] // width):
            cols = slice(c * width, (c + 1) * width)
            at = place_ref[h, :, cols]
            got = pick(packed, jnp.maximum(at, 0))
            out_ref[h, :, cols] = jnp.where(at >= 0, got, 0.0).astype(jnp.bfloat16)


def spread(packed, places):
    packs, count, features = places.shape
    width = packed.shape[1]
    return pl.pallas_call(
        functools.partial(spread_kernel, width),
        grid=(count // ROWS,),
        in_specs=[
            pl.BlockSpec((ROWS, width), lambda i: (i, 0)),
            pl.BlockSpec((packs, ROWS, features), lambda i: (0, i, 0)),
        ],
        out_specs=pl.BlockSpec((packs, ROWS, features), lambda i: (0, i, 0)),
        out_shape=jax.ShapeDtypeStruct(places.shape, jnp.bfloat16),
        cost_estimate=pl.CostEstimate(
            flops=places.size * 4, bytes_accessed=places.size * 6, transcendentals=0
        ),
        name="spread",
    )(packed, places)


def contract_rows(left, right):
    return lax.dot_general(
        left, right, (((0,), (0,)), ((), ())), preferred_element_type=jnp.float32
    )


def body(activations, top_lists, encoder_weight, encoder_bias, decoder_weight, decoder_bias):
    group_rows, hidden_dev = activations.shape
    feat_dev = encoder_weight.shape[1]
    top = top_lists.shape[1]
    shards, groups = lax.axis_size("feat"), lax.axis_size("tok")
    owner, group = lax.axis_index("feat"), lax.axis_index("tok")
    width = feat_dev // groups
    features = shards * width
    packs = width // top
    all_rows = group_rows * groups

    def own_weight(weight):
        columns = lax.dynamic_slice_in_dim(weight, group * width, width, 1)
        return lax.all_to_all(columns, "feat", split_axis=0, concat_axis=1, tiled=True)

    lists = lax.all_gather(top_lists, "tok", axis=0, tiled=True)
    inputs = lax.all_gather(activations, "tok", axis=0, tiled=True)
    encoder_own = own_weight(encoder_weight)
    decoder_own = own_weight(decoder_weight)

    in_block = lists % feat_dev
    local = jnp.where(
        in_block // width == group, lists // feat_dev * width + in_block % width, -1
    ).reshape(packs, all_rows // packs, top)
    packed_ids = jnp.stack(
        [
            jnp.pad(local[h], ((0, 0), (h * top, width - (h + 1) * top)), constant_values=-1)
            for h in range(packs)
        ]
    )
    places = place(local, features, width)
    bias = lax.dynamic_update_slice(
        jnp.zeros((1, features), jnp.float32),
        lax.dynamic_slice_in_dim(encoder_bias, group * width, width)[None, :],
        (0, owner * width),
    )

    def project_sum(rows, weight, offset):
        part = project(rows.reshape(packs, all_rows // packs, hidden_dev), weight, packed_ids, offset, width)
        return spread(lax.psum(part, "feat"), places).reshape(all_rows, features)

    codes = project_sum(inputs, encoder_own, bias)
    rebuilt = lax.psum_scatter(
        lax.dot_general(
            codes, decoder_own, (((1,), (1,)), ((), ())), preferred_element_type=jnp.float32
        ).astype(jnp.bfloat16),
        "tok",
        scatter_dimension=0,
        tiled=True,
    )
    own_bias = lax.dynamic_slice_in_dim(decoder_bias, owner * hidden_dev, hidden_dev)
    error_rows = (
        rebuilt.astype(jnp.float32) + own_bias - activations.astype(jnp.float32)
    ).astype(jnp.bfloat16)
    error = lax.all_gather(error_rows, "tok", axis=0, tiled=True)

    def send_home(gradient):
        tall = lax.all_to_all(gradient, "feat", split_axis=1, concat_axis=0, tiled=True)
        return lax.all_to_all(tall, "tok", split_axis=0, concat_axis=1, tiled=True)

    code_grads = project_sum(error, decoder_own, jnp.zeros_like(bias))
    decoder_grad = send_home(contract_rows(error, codes).astype(jnp.bfloat16))
    encoder_grad = send_home(contract_rows(inputs, code_grads).astype(jnp.bfloat16))
    return (encoder_grad.astype(jnp.float32), decoder_grad.astype(jnp.float32))


def solution(mesh):
    return jax.shard_map(
        body,
        mesh=mesh,
        in_specs=(
            P("tok", "feat"),
            P("tok", None),
            P(None, "feat"),
            P("feat"),
            P(None, "feat"),
            P(),
        ),
        out_specs=(P("tok", "feat"), P("tok", "feat")),
        check_vma=False,
    )
```

time: 640 us -> 519 us (0.81)
  waiting for transfers between devices: 421 us -> 228 us
  local copies, waits for them, and re-layouts: 139 us -> 38.5 us
  Pallas kernels: 0 us -> 99.5 us
  blocking collectives: 0 us -> 81.7 us
  matrix products: 48.7 us -> 24.6 us
  starting transfers between devices: 11.5 us -> 20.4 us
    reduce_scatter x1, waiting for transfers between devices: 240 us -> 39.5 us  [body(): lax.psum_scatter(lax.dot_general(codes, decoder_own, (((1,), (1,)), ((),...]
    unnamed x9 -> x15, local copies, waits for them, and re-layouts: 126 us -> 12.3 us
    psum x0 -> x2, waiting for transfers between devices: none -> 108 us  [project_sum(): return spread(lax.psum(part, 'feat'), places).reshape(all_rows, features)]
    all_gather x4 -> x2, waiting for transfers between devices: 134 us -> 31.6 us  [the longest x1 31.6 us: body(): error = lax.all_gather(error_rows, 'tok', axis=0, tiled=True)]
    pallas_call x0 -> x5, Pallas kernels: none -> 99.5 us  [the longest x1 58.1 us: place(): pl.pallas_call(functools.partial(place_kernel, width), grid=(packs, rows...]
    all_to_all x0 -> x2, blocking collectives: none -> 71.6 us  [the longest x1 44.4 us: send_home(): lax.all_to_all(gradient, 'feat', split_axis=1, concat_axis=0, tiled=True)]
    dot_general x3 -> x1, matrix products: 29.6 us -> 8.15 us  [body(): lax.dot_general(codes, decoder_own, (((1,), (1,)), ((), ())), preferred_e...]
    convert_element_type x0 -> x2, local copies, waits for them, and re-layouts: none -> 10.3 us  [body(): return (encoder_grad.astype(jnp.float32), decoder_grad.astype(jnp.float32))]
  transfers between devices with their start and end apart: 7 -> 9, of which waited for: 5 -> 6; matrix products, arithmetic and copies ran while one was open for 25% -> 7% of each run, Pallas kernels for 0% -> 19%
where the time goes in v1:
time: 519 us; the launch traced here: 517 us
  waiting for transfers between devices  228 us (44%)
  Pallas kernels  99.5 us (19%)
  blocking collectives  81.7 us (16%)
  local copies, waits for them, and re-layouts  38.5 us (7%)
  matrix products  24.6 us (5%)
  starting transfers between devices  20.4 us (4%)
  between operations  13.9 us (3%)
  other arithmetic  11 us (2%)
    psum x2, waiting for transfers between devices, project_sum(): return spread(lax.psum(part, 'feat'), places).reshape(all_rows, features)  108 us
    pallas_call x1, Pallas kernels, place(): pl.pallas_call(functools.partial(place_kernel, width), grid=(packs, rows...  58.1 us
    all_to_all x1, blocking collectives, send_home(): lax.all_to_all(gradient, 'feat', split_axis=1, concat_axis=0, tiled=True)  44.4 us
    reduce_scatter x1, waiting for transfers between devices, body(): lax.psum_scatter(lax.dot_general(codes, decoder_own, (((1,), (1,)), ((),...  39.5 us
    all_to_all x2, waiting for transfers between devices, own_weight(): lax.all_to_all(columns, 'feat', split_axis=0, concat_axis=1, tiled=True)  39 us
    all_gather x1, waiting for transfers between devices, body(): error = lax.all_gather(error_rows, 'tok', axis=0, tiled=True)  31.6 us
    all_to_all x1, blocking collectives, send_home(): return lax.all_to_all(tall, 'tok', split_axis=0, concat_axis=1, tiled=True)  27.3 us
    pallas_call x2, Pallas kernels, spread(): pl.pallas_call(functools.partial(spread_kernel, width), grid=(count // RO...  21.2 us
  transfers between devices with their start and end apart: 9, of which 6 were waited for; matrix products, arithmetic and copies ran while one was open for 7% of the time, Pallas kernels for 19%

profile of v1, /device:TPU:0, one launch (start us, length us, event | category | flops | bytes accessed | tf_op | source)
XLA Modules:
  0.0 517.5 jit_solution(6256630693027275775)
XLA Ops:
  7.2 2.9 constant_dynamic-slice_fusion.1
  10.0 7.3 %all-to-all-start = ((bf16[8,896,128]{2,1,0:T(8,128)(2,1)}), bf16[8,896,128]{2,1,0:T(8,128)(2,1)S(1)}, u32[]{:S(2)}, u32[]{:S(2)}) async-start(bf16[8,896,128]{2,1,0:T(8,128)(2,1)} %bitcast.58), calls=%async_computation | async-start | bytes 3670016 | tf_op jit(solution)/shard_map/all_to_all | solution.py:144
  18.1 2.9 constant_dynamic-slice_fusion
  20.9 39.0 %all-to-all-done = bf16[8,896,128]{2,1,0:T(8,128)(2,1)S(1)} async-done(((bf16[8,896,128]{2,1,0:T(8,128)(2,1)}), bf16[8,896,128]{2,1,0:T(8,128)(2,1)S(1)}, u32[]{:S(2)}, u32[]{:S(2)}) %all-to-all-start) | async-done | bytes 1835040 | tf_op jit(solution)/shard_map/all_to_all | solution.py:144
  61.2 3.6 all-to-all-start.1
  65.8 10.0 %all_gather.10 = s32[2048,64]{1,0:T(8,128)S(1)} all-gather(s32[512,64]{1,0:T(8,128)S(1)} %copy.15), channel_id=1, replica_groups=mesh['feat'=8,'tok'=4] {'tok'}, dimensions={0}, use_global_device_ids=true | all-gather | bytes 655360 | tf_op jit(solution)/shard_map/all_gather | solution.py:146
  75.8 1.9 fusion.3
  81.3 10.1 %project.2 = f32[1024,128]{1,0:T(8,128)} custom-call(bf16[2,1024,896]{2,1,0:T(8,128)(2,1)} %bitcast.64, bf16[896,1024]{1,0:T(8,128)(2,1)} %copy_bitcast_fusion.1.weight_ref, s32[2,1024,128]{2,1,0:T(8,128)} %pad_add_fusion.ids_ref, f32[1,1024]{1,0:T(1,128)} %copy-done.5), custom_call_target="tpu_custom_call" | custom-call | flops 3758096384 | bytes 5505024 | tf_op jit(solution)/shard_map/project/pallas_call | solution.py:77
  91.5 58.1 %place.1.place_ref = s32[2,1024,1024]{2,1,0:T(8,128)} custom-call(s32[2,1024,64]{2,1,0:T(8,128)} %bitcast.62), custom_call_target="tpu_custom_call" | custom-call | flops 2684354560 | bytes 8388608 | tf_op jit(solution)/shard_map/place/pallas_call | solution.py:41
  149.6 19.0 %all-reduce.5.cloned.1.call-done.packed_ref = f32[1024,128]{1,0:T(8,128)} async-done(((f32[1024,128]{1,0:T(8,128)}), f32[1024,128]{1,0:T(8,128)}) %all-reduce.5.cloned.1.call-update) | async-done | bytes 524304 | tf_op jit(solution)/shard_map/psum | solution.py:170
  168.6 10.6 %spread.2 = bf16[2,1024,1024]{2,1,0:T(8,128)(2,1)} custom-call(f32[1024,128]{1,0:T(8,128)} %all-reduce.5.cloned.1.call-done.packed_ref, s32[2,1024,1024]{2,1,0:T(8,128)} %place.1.place_ref), custom_call_target="tpu_custom_call" | custom-call | flops 8388608 | bytes 12582912 | tf_op jit(solution)/shard_map/spread/pallas_call | solution.py:109
  179.2 8.1 %convolution_convert_fusion = bf16[2048,896]{1,0:T(8,128)(2,1)} fusion(bf16[2048,1024]{1,0:T(8,128)(2,1)} %bitcast.59, bf16[8,896,128]{2,1,0:T(8,128)(2,1)S(1)} %all-to-all-done.1), kind=kOutput, calls=%fused_computation.2 | convolution fusion | flops 3759931392 | bytes 9699328 | tf_op jit(solution)/shard_map/dot_general | solution.py:174
  188.4 39.5 %reduce-scatter.2.cloned.1.call-done = bf16[512,896]{1,0:T(8,128)(2,1)} async-done(((bf16[2048,896]{1,0:T(8,128)(2,1)}), bf16[512,896]{1,0:T(8,128)(2,1)}) %reduce-scatter.2.cloned.1.call-update) | async-done | bytes 917520 | tf_op jit(solution)/shard_map/reduce_scatter | solution.py:173
  227.9 2.4 subtract_convert_fusion
  230.3 31.6 %all-gather.5.cloned.1.call-done = bf16[2048,896]{1,0:T(8,128)(2,1)} async-done(((bf16[512,896]{1,0:T(8,128)(2,1)}), bf16[2048,896]{1,0:T(8,128)(2,1)}) %all-gather.5.cloned.1.call-update) | async-done | bytes 3670032 | tf_op jit(solution)/shard_map/all_gather | solution.py:185
  262.0 7.3 %convert_bitcast_fusion.2 = bf16[112,8,8,128]{3,2,1,0:T(8,128)(2,1)S(1)} fusion(bf16[2048,896]{1,0:T(8,128)(2,1)} %all-gather.5.cloned.1.call-done, bf16[2048,1024]{1,0:T(8,128)(2,1)} %bitcast.60), kind=kOutput, calls=%fused_computation.6 | convolution fusion | flops 3759013888 | bytes 9699328 | tf_op jit(solution)/shard_map/dot_general | solution.py:126
  270.8 5.5 %all-to-all-start.4 = ((bf16[896,8,128]{2,0,1:T(8,128)(2,1)}), bf16[896,8,128]{2,0,1:T(8,128)(2,1)}, u32[]{:S(2)}, u32[]{:S(2)}) async-start(bf16[896,8,128]{2,0,1:T(8,128)(2,1)} %bitcast.56), calls=%async_computation.5 | async-start | bytes 3670016 | tf_op jit(solution)/shard_map/all_to_all | solution.py:188
  278.5 10.1 %project.3 = f32[1024,128]{1,0:T(8,128)} custom-call(bf16[2,1024,896]{2,1,0:T(8,128)(2,1)} %bitcast.65, bf16[896,1024]{1,0:T(8,128)(2,1)} %copy_bitcast_fusion.weight_ref, s32[2,1024,128]{2,1,0:T(8,128)} %pad_add_fusion.ids_ref, f32[1,1024]{1,0:T(1,128)} %broadcast_3_bias_ref.2.bias_ref), custom_call_target="tpu_custom_call" | custom-call | flops 3758096384 | bytes 5505024 | tf_op jit(solution)/shard_map/project/pallas_call | solution.py:77
  288.7 89.0 %all-reduce.7.cloned.1.call-done.packed_ref = f32[1024,128]{1,0:T(8,128)} async-done(((f32[1024,128]{1,0:T(8,128)}), f32[1024,128]{1,0:T(8,128)}) %all-reduce.7.cloned.1.call-update) | async-done | bytes 524304 | tf_op jit(solution)/shard_map/psum | solution.py:170
  377.6 10.6 %spread.3 = bf16[2,1024,1024]{2,1,0:T(8,128)(2,1)} custom-call(f32[1024,128]{1,0:T(8,128)} %all-reduce.7.cloned.1.call-done.packed_ref, s32[2,1024,1024]{2,1,0:T(8,128)} %place.1.place_ref), custom_call_target="tpu_custom_call" | custom-call | flops 8388608 | bytes 12582912 | tf_op jit(solution)/shard_map/spread/pallas_call | solution.py:109
  388.2 9.1 %convolution_convert_fusion.1 = bf16[1024,896]{1,0:T(8,128)(2,1)} fusion(bf16[2048,1024]{1,0:T(8,128)(2,1)} %bitcast.61, bf16[2048,896]{1,0:T(8,128)(2,1)} %all-gather.3.cloned.1.call-done), kind=kOutput, calls=%fused_computation.8 | convolution fusion | flops 3759013888 | bytes 9699328 | tf_op jit(solution)/shard_map/dot_general | solution.py:126
  397.3 3.2 copy.17
  400.5 44.4 %all_to_all.96 = bf16[896,8,128]{2,0,1:T(8,128)(2,1)} all-to-all(bf16[896,8,128]{2,0,1:T(8,128)(2,1)S(1)} %copy.17), channel_id=1, replica_groups=mesh['feat'=8,'tok'=4] {'feat'}, dimensions={1} | all-to-all | bytes 3670016 | tf_op jit(solution)/shard_map/all_to_all | solution.py:188
  444.9 27.3 %all_to_all.97 = bf16[4,1792,128]{2,1,0:T(8,128)(2,1)} all-to-all(bf16[4,1792,128]{2,1,0:T(8,128)(2,1)} %bitcast.19), channel_id=1, replica_groups=mesh['feat'=8,'tok'=4] {'tok'}, dimensions={0} | all-to-all | bytes 3670016 | tf_op jit(solution)/shard_map/all_to_all | solution.py:189
  472.2 3.6 all-to-all-start.3
  475.8 3.6 convert_bitcast_fusion
  479.3 5.1 copy.20
  484.5 5.1 copy.22
  489.6 9.0 %all-to-all-done.3 = bf16[4,1792,128]{2,1,0:T(8,128)(2,1)S(1)} async-done(((bf16[4,1792,128]{2,1,0:T(8,128)(2,1)}), bf16[4,1792,128]{2,1,0:T(8,128)(2,1)S(1)}, u32[]{:S(2)}, u32[]{:S(2)}) %all-to-all-start.3) | async-done | bytes 1835040 | tf_op jit(solution)/shard_map/all_to_all | solution.py:189
  498.6 2.1 convert_bitcast_fusion.1
  500.7 5.2 copy.18
  505.8 5.1 copy.21
  (36 shorter events, 11.3 us)
Async XLA Ops:
  10.0 49.9 %all-to-all-start = ((bf16[8,896,128]{2,1,0:T(8,128)(2,1)}), bf16[8,896,128]{2,1,0:T(8,128)(2,1)S(1)}, u32[]{:S(2)}, u32[]{:S(2)}) async-start(bf16[8,896,128]{2,1,0:T(8,128)(2,1)} %bitcast.58), calls=%async_computation | async-start | bytes 3670016 | tf_op jit(solution)/shard_map/all_to_all | solution.py:144
  17.3 64.0 %all-gather.3.cloned.1.call-start = ((), (), s32[]{:S(2)}) async-start(), calls=%async_computation.7 | async-start | bytes 4587520 | tf_op jit(solution)/shard_map/all_gather | solution.py:147
  60.0 1.2 copy-start
  60.0 4.9 copy-start.4
  61.2 118.0 %all-to-all-start.1 = ((bf16[8,896,128]{2,1,0:T(8,128)(2,1)}), bf16[8,896,128]{2,1,0:T(8,128)(2,1)S(1)}, u32[]{:S(2)}, u32[]{:S(2)}) async-start(bf16[8,896,128]{2,1,0:T(8,128)(2,1)} %bitcast.57), calls=%async_computation.1 | async-start | bytes 3670016 | tf_op jit(solution)/shard_map/all_to_all | solution.py:144
  64.8 103.8 %all-reduce.5.cloned.1.call-start = ((), (), s32[]{:S(2)}) async-start(), calls=%async_computation.8 | async-start | bytes 1048576 | tf_op jit(solution)/shard_map/psum | solution.py:170
  65.8 12.0 %copy-start.5 = (f32[1,1024]{1,0:T(1,128)}, f32[1,1024]{1,0:T(1,128)S(1)}, u32[]{:S(2)}) copy-start(f32[1,1024]{1,0:T(1,128)S(1)} %constant_dynamic-update-slice_fusion.bias_ref) | copy-start | bytes 12292
  77.7 1.1 copy-start.2
  77.8 2.0 copy-start.1
  91.5 136.4 %reduce-scatter.2.cloned.1.call-start = ((), (), s32[]{:S(2)}) async-start(), calls=%async_computation.9 | async-start | bytes 4587520 | tf_op jit(solution)/shard_map/reduce_scatter | solution.py:173
  187.3 40.6 %copy-start.3 = (bf16[512,896]{1,0:T(8,128)(2,1)S(1)}, bf16[512,896]{1,0:T(8,128)(2,1)}, u32[]{:S(2)}) copy-start(bf16[512,896]{1,0:T(8,128)(2,1)} %param.6) | copy-start | bytes 2752516
  187.4 74.6 %all-gather.5.cloned.1.call-start = ((), (), s32[]{:S(2)}) async-start(), calls=%async_computation.10 | async-start | bytes 4587520 | tf_op jit(solution)/shard_map/all_gather | solution.py:185
  270.8 129.7 %all-to-all-start.4 = ((bf16[896,8,128]{2,0,1:T(8,128)(2,1)}), bf16[896,8,128]{2,0,1:T(8,128)(2,1)}, u32[]{:S(2)}, u32[]{:S(2)}) async-start(bf16[896,8,128]{2,0,1:T(8,128)(2,1)} %bitcast.56), calls=%async_computation.5 | async-start | bytes 3670016 | tf_op jit(solution)/shard_map/all_to_all | solution.py:188
  276.4 101.3 %all-reduce.7.cloned.1.call-start = ((), (), s32[]{:S(2)}) async-start(), calls=%async_computation.11 | async-start | bytes 1048576 | tf_op jit(solution)/shard_map/psum | solution.py:170
  472.2 26.4 %all-to-all-start.3 = ((bf16[4,1792,128]{2,1,0:T(8,128)(2,1)}), bf16[4,1792,128]{2,1,0:T(8,128)(2,1)S(1)}, u32[]{:S(2)}, u32[]{:S(2)}) async-start(bf16[4,1792,128]{2,1,0:T(8,128)(2,1)} %bitcast.15), calls=%async_computation.4 | async-start | bytes 3670016 | tf_op jit(solution)/shard_map/all_to_all | solution.py:189
Sparse Core Ops, SparseCore 0:
  19.7 32.8 all-gather.2
  91.6 76.9 all-reduce.4
  187.5 40.3 reduce-scatter.1
  230.4 31.4 all-gather.4
  288.8 88.8 all-reduce.6
